TPU v7x, 32 devices: a whole 2x2x4 slice. The times are simulated.
32 devices in a mesh: dop: 2 (over y), rng: 16 (over z, x, core).
Axes of the slice: x: 2, y: 2, z: 4, core: 2. Of those that a mesh axis runs over, the one named last changes fastest.
Arguments:
- radar_cube: bfloat16 [2, 128, 1024, 512], P(None, 'dop', 'rng'), may hold values from -40 to 40
- train_gates: int32 [2, 768], P('dop', 'rng'), may hold values from 0 to 63, as said below
- look_angles: int32 [2, 8], P('dop'), may hold values from 0 to 255
Outputs:
- filtered: float32 [2, 2, 8, 1024], P(None, 'dop', None, 'rng')
Inputs may be any that keep to these rules, and one draw needn't show every extreme that they name: `train_gates`: entries k * 48 to (k + 1) * 48 - 1 of a bin's row list in increasing order the gates of the k-th block of 64 consecutive range gates, counted from that block's first gate, that lie outside one run of 16 consecutive gates of the block.
All inputs are finite; a program needn't handle non-finite values.
Results may differ from a plain program's by a relative error of at most 0.014.
The roundings to bfloat16 on the way count: a program that leaves them out, or rounds other values in their place, can miss the bound.
Values may be sent and summed in bfloat16 or wider, within the bound.
No kernel may reach another device: no remote copies, remote signals or barrier semaphores. Data moves between devices by JAX's collectives and lax.ppermute only.
A program may use at most 64 MiB of HBM per device.

v0:
```python
import math
import jax
import jax.numpy as jnp
from jax import lax
from jax.sharding import PartitionSpec as P

P_SIZE = 128
NANG = 256
load_eps = 1e-05


def doppler_table(bin_count, pulses):
    bin_freq = jnp.arange(bin_count, dtype=jnp.int32) * (pulses // bin_count)
    pulse_index = jnp.arange(pulses, dtype=jnp.int32)
    phase = (bin_freq[:, None] * pulse_index[None, :] % pulses).astype(jnp.float32) * (
        2.0 * math.pi / pulses
    )
    cosine = jnp.cos(phase).astype(jnp.bfloat16)
    sine = jnp.sin(phase).astype(jnp.bfloat16)
    upper = jnp.concatenate([cosine, sine], 1)
    lower = jnp.concatenate([-sine, cosine], 1)
    return jnp.concatenate([upper, lower], 0)


def gram_terms(train_rows):
    real_part = train_rows[0]
    imag_part = train_rows[1]
    contract = (((0,), (0,)), ((), ()))
    stacked = jnp.concatenate([real_part, imag_part], 0)
    power_sum = lax.dot_general(stacked, stacked, contract, preferred_element_type=jnp.float32)
    left_rows = jnp.concatenate([real_part, -imag_part], 0)
    right_rows = jnp.concatenate([imag_part, real_part], 0)
    cross_sum = lax.dot_general(left_rows, right_rows, contract, preferred_element_type=jnp.float32)
    return (power_sum, cross_sum)


def solve_weights(power_sum, cross_sum, look_row, train_count, angle_count):
    channels = power_sum.shape[0]
    top_half = jnp.concatenate([power_sum, cross_sum], 1)
    bottom_half = jnp.concatenate([cross_sum.T, power_sum], 1)
    covariance = jnp.concatenate([top_half, bottom_half], 0) / train_count
    loading = load_eps * jnp.trace(covariance) / (2 * channels)
    covariance = covariance + loading * jnp.eye(2 * channels, dtype=jnp.float32)
    factor = jnp.linalg.cholesky(covariance)
    channel_index = jnp.arange(channels, dtype=jnp.int32)
    slope = 2 * look_row + 1 - angle_count
    modulus = channel_index[:, None] * slope[None, :] % (2 * angle_count)
    phase = modulus.astype(jnp.float32) * (math.pi / angle_count)
    steering = jnp.concatenate([jnp.cos(phase), jnp.sin(phase)], 0)
    whitened = jax.scipy.linalg.solve_triangular(factor, steering, lower=True)
    lengths = jnp.sqrt(jnp.sum(whitened * whitened, axis=0))
    weights = jax.scipy.linalg.solve_triangular(
        factor, whitened / lengths[None, :], trans=1, lower=True
    )
    return weights.astype(jnp.bfloat16)


def filter_gates(spectrum, weights):
    direct = jnp.concatenate([spectrum[0], spectrum[1]], 1)
    rotated = jnp.concatenate([-spectrum[1], spectrum[0]], 1)
    contract = (((0,), (1,)), ((), ()))
    real_out = lax.dot_general(weights, direct, contract, preferred_element_type=jnp.float32)
    imag_out = lax.dot_general(weights, rotated, contract, preferred_element_type=jnp.float32)
    return jnp.stack([real_out, imag_out])


def pack_terms(power_part, cross_part, lower_mask):
    return jnp.where(lower_mask, power_part, cross_part)


def unpack_terms(packed, row_index, col_index):
    lower_mask = row_index >= col_index
    lower_part = jnp.where(lower_mask, packed, 0.0)
    strict_lower = jnp.where(row_index > col_index, packed, 0.0)
    power_sum = lower_part + strict_lower.T
    upper_part = jnp.where(lower_mask, 0.0, packed)
    cross_sum = upper_part - upper_part.T
    return (power_sum, cross_sum)


def on_device(radar_cube, train_gates, look_angles):
    dop_count = lax.axis_size("dop")
    rng_count = lax.axis_size("rng")
    bin_local = train_gates.shape[0]
    bin_count = dop_count * bin_local
    dft_table = doppler_table(bin_count, P_SIZE)
    norm_scale = 1.0 / math.sqrt(P_SIZE)
    segment = lax.all_to_all(radar_cube, "dop", split_axis=2, concat_axis=1, tiled=True)
    flattened = segment.reshape(2 * P_SIZE, -1)
    spectral = (
        jnp.dot(dft_table, flattened, preferred_element_type=jnp.float32) * norm_scale
    ).astype(jnp.bfloat16)
    spectral = spectral.reshape(2, bin_count, segment.shape[2], segment.shape[3])
    binned = lax.all_to_all(spectral, "dop", split_axis=1, concat_axis=2, tiled=True)
    channels = binned.shape[3]
    train_count = train_gates.shape[1] * rng_count
    row_index = lax.broadcasted_iota(jnp.int32, (channels, channels), 0)
    col_index = lax.broadcasted_iota(jnp.int32, (channels, channels), 1)
    lower_mask = row_index >= col_index
    rows = jnp.take(binned[:, 0], train_gates[0], axis=1)
    power_part, cross_part = gram_terms(rows)
    packed_all = jnp.stack([pack_terms(power_part, cross_part, lower_mask)])
    summed = lax.psum(packed_all, "rng")

    def unpack_one(packed):
        return unpack_terms(packed, row_index, col_index)

    power_all, cross_all = jax.vmap(unpack_one)(summed)

    def solve_one(inputs):
        return solve_weights(inputs[0], inputs[1], inputs[2], train_count, NANG)

    weights_all = lax.map(solve_one, (power_all, cross_all, look_angles))
    outputs = [filter_gates(binned[:, 0], weights_all[0])]
    return jnp.stack(outputs, 1)


def solution(mesh):
    placed = (P(None, "dop", "rng", None), P("dop", "rng"), P("dop", None))
    return jax.shard_map(
        on_device,
        mesh=mesh,
        in_specs=placed,
        out_specs=P(None, "dop", None, "rng"),
        check_vma=False,
    )
```

profile of v0, /device:TPU:0, one launch (start us, length us, event | category | flops | bytes accessed | tf_op | source)
XLA Modules:
  0.0 629.6 jit_solution(5859860382280964349)
XLA Ops:
  6.5 11.3 %copy.107 = bf16[2,64,64,512]{3,1,0,2:T(8,128)(2,1)} copy(bf16[2,64,64,512]{3,2,1,0:T(8,128)(2,1)} %param.3) | data formatting | bytes 16777216 | tf_op args[0]
  17.9 7.2 %all-to-all-start = ((bf16[2,64,64,512]{3,1,0,2:T(8,128)(2,1)}), bf16[2,64,64,512]{3,1,0,2:T(8,128)(2,1)}, u32[]{:S(2)}, u32[]{:S(2)}) async-start(bf16[2,64,64,512]{3,1,0,2:T(8,128)(2,1)} %copy.107), calls=%async_computation | async-start | bytes 16777216 | tf_op jit(solution)/shard_map/all_to_all | solution.py:88
  26.1 92.9 %all-to-all-done = bf16[2,64,64,512]{3,1,0,2:T(8,128)(2,1)} async-done(((bf16[2,64,64,512]{3,1,0,2:T(8,128)(2,1)}), bf16[2,64,64,512]{3,1,0,2:T(8,128)(2,1)}, u32[]{:S(2)}, u32[]{:S(2)}) %all-to-all-start) | async-done | bytes 8388640 | tf_op jit(solution)/shard_map/all_to_all | solution.py:88
  119.0 11.4 %copy.108 = bf16[2,64,2,32,512]{4,3,1,2,0:T(8,128)(2,1)} copy(bf16[2,64,2,32,512]{4,1,0,3,2:T(8,128)(2,1)} %bitcast.1) | data formatting | bytes 16777216 | tf_op jit(solution)/shard_map/all_to_all | solution.py:88
  130.4 15.6 %copy.155 = bf16[32,8,32,512]{3,1,2,0:T(8,128)(2,1)} copy(bf16[32,8,32,512]{3,2,1,0:T(8,128)(2,1)} %bitcast.183) | data formatting | bytes 16777216
  146.0 4.6 fusion
  151.3 3.4 all-to-all-start.1
  154.7 4.4 all-to-all-done.1
  162.1 94.4 %all-reduce.3.cloned.1.call-done = f32[1,512,512]{2,1,0:T(8,128)} async-done(((f32[1,512,512]{2,1,0:T(8,128)}), f32[1,512,512]{2,1,0:T(8,128)}) %all-reduce.3.cloned.1.call-update) | async-done | bytes 1048592 | tf_op jit(solution)/shard_map/psum | solution.py:103
  260.7 3.3 fusion.11
  264.0 1.6 copy.116
  267.1 2.6 select_add_fusion
  269.7 5.7 copy.117
  275.4 3.2 fusion.1
  278.6 1.9 copy-done.1
  280.6 11.7 %cholesky.222 = f32[128,128]{1,0:T(8,128)S(1)} custom-call(f32[128,128]{1,0:T(8,128)S(1)} %cholesky.577), custom_call_target="Cholesky" | custom-call | tf_op jit(solution)/shard_map/while/body/eval_jaxpr/jit(cholesky)/cholesky | solution.py:44
  292.3 9.8 %custom-call.82 = f32[1,128,128]{1,2,0:T(8,128)S(1)} custom-call(f32[1,128,128]{2,1,0:T(8,128)S(1)} %get-tuple-element.79), custom_call_target="InvertDiagBlocksLowerTriangular" | custom-call | tf_op jit(solution)/shard_map/while/body/eval_jaxpr/jit(cholesky)/cholesky | solution.py:44
  305.3 11.7 %cholesky.243 = f32[128,128]{1,0:T(8,128)S(1)} custom-call(f32[128,128]{1,0:T(8,128)S(1)} %cholesky.581), custom_call_target="Cholesky" | custom-call | tf_op jit(solution)/shard_map/while/body/eval_jaxpr/jit(cholesky)/cholesky | solution.py:44
  317.6 9.8 %custom-call.83 = f32[1,128,128]{1,2,0:T(8,128)S(1)} custom-call(f32[1,128,128]{2,1,0:T(8,128)S(1)} %get-tuple-element.77), custom_call_target="InvertDiagBlocksLowerTriangular" | custom-call | tf_op jit(solution)/shard_map/while/body/eval_jaxpr/jit(cholesky)/cholesky | solution.py:44
  328.5 2.0 copy-done
  330.5 2.4 convolution_subtract_fusion.1
  332.9 11.7 %cholesky.466 = f32[128,128]{1,0:T(8,128)S(1)} custom-call(f32[128,128]{1,0:T(8,128)S(1)} %cholesky.586), custom_call_target="Cholesky" | custom-call | tf_op jit(solution)/shard_map/while/body/eval_jaxpr/jit(cholesky)/cholesky | solution.py:44
  345.4 9.8 %custom-call.84 = f32[1,128,128]{1,2,0:T(8,128)S(1)} custom-call(f32[1,128,128]{2,1,0:T(8,128)S(1)} %get-tuple-element.75), custom_call_target="InvertDiagBlocksLowerTriangular" | custom-call | tf_op jit(solution)/shard_map/while/body/eval_jaxpr/jit(cholesky)/cholesky | solution.py:44
  356.5 3.3 convolution_subtract_fusion.2
  359.8 11.7 %cholesky.485 = f32[128,128]{1,0:T(8,128)S(1)} custom-call(f32[128,128]{1,0:T(8,128)S(1)} %cholesky.591), custom_call_target="Cholesky" | custom-call | tf_op jit(solution)/shard_map/while/body/eval_jaxpr/jit(cholesky)/cholesky | solution.py:44
  372.3 9.8 %custom-call.85 = f32[1,128,128]{1,2,0:T(8,128)S(1)} custom-call(f32[1,128,128]{2,1,0:T(8,128)S(1)} %get-tuple-element.73), custom_call_target="InvertDiagBlocksLowerTriangular" | custom-call | tf_op jit(solution)/shard_map/while/body/eval_jaxpr/jit(cholesky)/cholesky | solution.py:44
  383.2 3.1 convolution_subtract_fusion.3
  386.4 12.1 %cholesky.504 = f32[128,128]{1,0:T(8,128)S(1)} custom-call(f32[128,128]{1,0:T(8,128)S(1)} %cholesky.596), custom_call_target="Cholesky" | custom-call | tf_op jit(solution)/shard_map/while/body/eval_jaxpr/jit(cholesky)/cholesky | solution.py:44
  399.3 9.8 %custom-call.86 = f32[1,128,128]{1,2,0:T(8,128)S(1)} custom-call(f32[1,128,128]{2,1,0:T(8,128)S(1)} %get-tuple-element.71), custom_call_target="InvertDiagBlocksLowerTriangular" | custom-call | tf_op jit(solution)/shard_map/while/body/eval_jaxpr/jit(cholesky)/cholesky | solution.py:44
  410.2 3.1 convolution_subtract_fusion.4
  413.3 11.7 %cholesky.524 = f32[128,128]{1,0:T(8,128)S(1)} custom-call(f32[128,128]{1,0:T(8,128)S(1)} %cholesky.601), custom_call_target="Cholesky" | custom-call | tf_op jit(solution)/shard_map/while/body/eval_jaxpr/jit(cholesky)/cholesky | solution.py:44
  425.8 9.8 %custom-call.87 = f32[1,128,128]{1,2,0:T(8,128)S(1)} custom-call(f32[1,128,128]{2,1,0:T(8,128)S(1)} %get-tuple-element.69), custom_call_target="InvertDiagBlocksLowerTriangular" | custom-call | tf_op jit(solution)/shard_map/while/body/eval_jaxpr/jit(cholesky)/cholesky | solution.py:44
  436.6 2.8 convolution_subtract_fusion.5
  439.4 11.7 %cholesky.544 = f32[128,128]{1,0:T(8,128)S(1)} custom-call(f32[128,128]{1,0:T(8,128)S(1)} %cholesky.606), custom_call_target="Cholesky" | custom-call | tf_op jit(solution)/shard_map/while/body/eval_jaxpr/jit(cholesky)/cholesky | solution.py:44
  451.9 9.8 %custom-call.88 = f32[1,128,128]{1,2,0:T(8,128)S(1)} custom-call(f32[1,128,128]{2,1,0:T(8,128)S(1)} %get-tuple-element.67), custom_call_target="InvertDiagBlocksLowerTriangular" | custom-call | tf_op jit(solution)/shard_map/while/body/eval_jaxpr/jit(cholesky)/cholesky | solution.py:44
  462.7 2.1 convolution_subtract_fusion.6
  464.8 11.7 %cholesky.562 = f32[128,128]{1,0:T(8,128)S(1)} custom-call(f32[128,128]{1,0:T(8,128)S(1)} %convolution_subtract_fusion.6), custom_call_target="Cholesky" | custom-call | tf_op jit(solution)/shard_map/while/body/eval_jaxpr/jit(cholesky)/cholesky | solution.py:44
  487.6 4.8 select_select_fusion
  492.4 28.5 %while.1 = (s32[]{:T(128)}, f32[1024,1024]{0,1:T(8,128)}, s32[8,2]{0,1:T(2,128)S(1)}, f32[8,128,128]{2,1,0:T(8,128)}, s32[]{:T(128)}) while((s32[]{:T(128)}, f32[1024,1024]{0,1:T(8,128)}, s32[8,2]{0,1:T(2,128)S(1)}, f32[8,128,128]{2,1,0:T(8,128)}, s32[]{:T(128)}) %tuple.66), condition=%wide.while_cond, body=%wide.while_body.sunk | while | flops 2 | bytes 393829 | solution.py:52
  493.0 2.2 dynamic-slice.7
  496.6 2.2 dynamic-slice.7
  500.2 2.2 dynamic-slice.7
  503.8 2.2 dynamic-slice.7
  507.3 2.2 dynamic-slice.7
  510.9 2.2 dynamic-slice.7
  514.5 2.2 dynamic-slice.7
  518.0 2.2 dynamic-slice.7
  520.9 79.6 %custom-call.89 = f32[8,128,128]{1,2,0:T(8,128)S(1)} custom-call(f32[8,128,128]{2,1,0:T(8,128)} %get-tuple-element.27), custom_call_target="InvertDiagBlocksLowerTriangular" | custom-call | tf_op jit(solution)/shard_map/while/body/eval_jaxpr/jit(_solve_triangular)/triangular_solve | solution.py:52
  (180 shorter events, 62.3 us)
Async XLA Ops:
  17.9 7.7 %copy-start.4 = (s32[1,48]{1,0:T(1,128)S(1)}, s32[1,48]{1,0:T(1,128)}, u32[]{:S(2)}) copy-start(s32[1,48]{1,0:T(1,128)} %param.4) | copy-start | bytes 580
  17.9 7.9 %copy-start.5 = (s32[1,8]{1,0:T(1,128)S(1)}, s32[1,8]{1,0:T(1,128)}, u32[]{:S(2)}) copy-start(s32[1,8]{1,0:T(1,128)} %param.5) | copy-start | bytes 100
  17.9 101.1 %all-to-all-start = ((bf16[2,64,64,512]{3,1,0,2:T(8,128)(2,1)}), bf16[2,64,64,512]{3,1,0,2:T(8,128)(2,1)}, u32[]{:S(2)}, u32[]{:S(2)}) async-start(bf16[2,64,64,512]{3,1,0,2:T(8,128)(2,1)} %copy.107), calls=%async_computation | async-start | bytes 16777216 | tf_op jit(solution)/shard_map/all_to_all | solution.py:88
  151.3 7.8 %all-to-all-start.1 = ((bf16[2,2,32,512]{3,2,0,1:T(8,128)(2,1)}), bf16[2,2,32,512]{3,2,0,1:T(8,128)(2,1)S(1)}, u32[]{:S(2)}, u32[]{:S(2)}) async-start(bf16[2,2,32,512]{3,2,0,1:T(8,128)(2,1)} %copy.109), calls=%async_computation.1 | async-start | bytes 262144 | tf_op jit(solution)/shard_map/all_to_all | solution.py:94
  154.6 101.8 %all-reduce.3.cloned.1.call-start = ((), (), s32[]{:S(2)}) async-start(), calls=%async_computation.2 | async-start | bytes 2097152 | tf_op jit(solution)/shard_map/psum | solution.py:103
  256.5 2.8 copy-start.2
  257.9 1.3 copy-start.3
  278.6 1.9 copy-start.1
  328.5 2.0 copy-start
Sparse Core Ops, SparseCore 0:
  162.2 94.2 all-reduce.2
where the time goes:
time: 636 us; the launch traced here: 630 us
  other arithmetic  266 us (42%)
  waiting for transfers between devices  192 us (30%)
  local copies, waits for them, and re-layouts  88.4 us (14%)
  matrix products  52.9 us (8%)
  between operations  19.9 us (3%)
  starting transfers between devices  10.6 us (2%)
    another operation x31, other arithmetic, solve_weights(): factor = jnp.linalg.cholesky(covariance)  168 us
    psum x1, waiting for transfers between devices, on_device(): summed = lax.psum(packed_all, 'rng')  94.4 us
    all_to_all x1, waiting for transfers between devices, on_device(): lax.all_to_all(radar_cube, 'dop', split_axis=2, concat_axis=1, tiled=True)  92.9 us
    another operation x4, other arithmetic, solve_weights(): jax.scipy.linalg.solve_triangular(factor, whitened / lengths[None, :], tr...  84.4 us
    unnamed x29, local copies, waits for them, and re-layouts  31 us
    another operation x40, local copies, waits for them, and re-layouts  28.4 us
    another operation x14, matrix products, solve_weights(): factor = jnp.linalg.cholesky(covariance)  25.9 us
  transfers between devices with their start and end apart: 3, of which 3 were waited for; matrix products, arithmetic and copies ran while one was open for 0% of the time, Pallas kernels for 0%

commit v1 on v0

--- a/solution.py
+++ b/solution.py
@@ -100,7 +100,7 @@
     rows = jnp.take(binned[:, 0], train_gates[0], axis=1)
     power_part, cross_part = gram_terms(rows)
     packed_all = jnp.stack([pack_terms(power_part, cross_part, lower_mask)])
-    summed = lax.psum(packed_all, "rng")
+    summed = jnp.sum(lax.all_gather(packed_all, "rng"), axis=0)
 
     def unpack_one(packed):
         return unpack_terms(packed, row_index, col_index)

time: 636 us -> 677 us (1.064)
  waiting for transfers between devices: 192 us -> 224 us
    all_gather x0 -> x1, waiting for transfers between devices: none -> 126 us  [on_device(): summed = jnp.sum(lax.all_gather(packed_all, 'rng'), axis=0)]
    psum x1 -> x0, waiting for transfers between devices: 94.4 us -> none  [on_device(): summed = lax.psum(packed_all, 'rng')]
    reduce_sum x0 -> x1, other arithmetic: none -> 7.91 us  [on_device(): summed = jnp.sum(lax.all_gather(packed_all, 'rng'), axis=0)]
    unnamed x29 -> x25, local copies, waits for them, and re-layouts: 31 us -> 29 us
where the time goes in v1:
time: 677 us; the launch traced here: 671 us
  other arithmetic  272 us (40%)
  waiting for transfers between devices  224 us (33%)
  local copies, waits for them, and re-layouts  89.8 us (13%)
  matrix products  54 us (8%)
  between operations  19.9 us (3%)
  starting transfers between devices  10.6 us (2%)
    another operation x31, other arithmetic, solve_weights(): factor = jnp.linalg.cholesky(covariance)  168 us
    all_gather x1, waiting for transfers between devices, on_device(): summed = jnp.sum(lax.all_gather(packed_all, 'rng'), axis=0)  126 us
    all_to_all x1, waiting for transfers between devices, on_device(): lax.all_to_all(radar_cube, 'dop', split_axis=2, concat_axis=1, tiled=True)  93.6 us
    another operation x4, other arithmetic, solve_weights(): jax.scipy.linalg.solve_triangular(factor, whitened / lengths[None, :], tr...  84.4 us
    unnamed x25, local copies, waits for them, and re-layouts  29 us
    another operation x40, local copies, waits for them, and re-layouts  28.4 us
    another operation x14, matrix products, solve_weights(): factor = jnp.linalg.cholesky(covariance)  27 us
  transfers between devices with their start and end apart: 3, of which 3 were waited for; matrix products, arithmetic and copies ran while one was open for 0% of the time, Pallas kernels for 0%

profile of v1, /device:TPU:0, one launch (start us, length us, event | category | flops | bytes accessed | tf_op | source)
XLA Modules:
  0.0 671.3 jit_solution(929261290024821387)
XLA Ops:
  6.5 11.3 %copy.107 = bf16[2,64,64,512]{3,1,0,2:T(8,128)(2,1)} copy(bf16[2,64,64,512]{3,2,1,0:T(8,128)(2,1)} %param.3) | data formatting | bytes 16777216 | tf_op args[0]
  17.9 7.2 %all-to-all-start = ((bf16[2,64,64,512]{3,1,0,2:T(8,128)(2,1)}), bf16[2,64,64,512]{3,1,0,2:T(8,128)(2,1)}, u32[]{:S(2)}, u32[]{:S(2)}) async-start(bf16[2,64,64,512]{3,1,0,2:T(8,128)(2,1)} %copy.107), calls=%async_computation | async-start | bytes 16777216 | tf_op jit(solution)/shard_map/all_to_all | solution.py:88
  25.4 93.6 %all-to-all-done = bf16[2,64,64,512]{3,1,0,2:T(8,128)(2,1)} async-done(((bf16[2,64,64,512]{3,1,0,2:T(8,128)(2,1)}), bf16[2,64,64,512]{3,1,0,2:T(8,128)(2,1)}, u32[]{:S(2)}, u32[]{:S(2)}) %all-to-all-start) | async-done | bytes 8388640 | tf_op jit(solution)/shard_map/all_to_all | solution.py:88
  119.0 11.4 %copy.108 = bf16[2,64,2,32,512]{4,3,1,2,0:T(8,128)(2,1)} copy(bf16[2,64,2,32,512]{4,1,0,3,2:T(8,128)(2,1)} %bitcast.1) | data formatting | bytes 16777216 | tf_op jit(solution)/shard_map/all_to_all | solution.py:88
  130.4 15.6 %copy.156 = bf16[32,8,32,512]{3,1,2,0:T(8,128)(2,1)} copy(bf16[32,8,32,512]{3,2,1,0:T(8,128)(2,1)} %bitcast.185) | data formatting | bytes 16777216
  146.0 4.6 fusion
  151.3 3.4 all-to-all-start.1
  154.7 4.4 all-to-all-done.1
  162.8 126.3 %all-gather.3.cloned.1.call-done = f32[8192,512]{1,0:T(8,128)} async-done(((f32[512,512]{1,0:T(8,128)}), f32[8192,512]{1,0:T(8,128)}) %all-gather.3.cloned.1.call-update) | async-done | bytes 16777232 | tf_op jit(solution)/shard_map/all_gather | solution.py:103
  289.1 7.9 %reduce.65 = f32[512,512]{1,0:T(8,128)S(1)} reduce(f32[16,512,512]{2,1,0:T(8,128)} %bitcast.186, f32[]{:T(128)} %constant.370.clone.1), dimensions={0}, to_apply=%region_0.1 | reduce | flops 3932160 | bytes 17825796 | tf_op jit(solution)/shard_map/reduce_sum | solution.py:103
  299.9 3.3 fusion.10
  306.3 2.6 select_add_fusion
  308.9 5.7 copy.117
  314.6 3.2 fusion.1
  317.8 1.9 copy-done
  319.8 11.7 %cholesky.222 = f32[128,128]{1,0:T(8,128)S(1)} custom-call(f32[128,128]{1,0:T(8,128)S(1)} %cholesky.577), custom_call_target="Cholesky" | custom-call | tf_op jit(solution)/shard_map/while/body/eval_jaxpr/jit(cholesky)/cholesky | solution.py:44
  331.5 9.8 %custom-call.82 = f32[1,128,128]{1,2,0:T(8,128)S(1)} custom-call(f32[1,128,128]{2,1,0:T(8,128)S(1)} %get-tuple-element.79), custom_call_target="InvertDiagBlocksLowerTriangular" | custom-call | tf_op jit(solution)/shard_map/while/body/eval_jaxpr/jit(cholesky)/cholesky | solution.py:44
  344.5 11.7 %cholesky.243 = f32[128,128]{1,0:T(8,128)S(1)} custom-call(f32[128,128]{1,0:T(8,128)S(1)} %cholesky.581), custom_call_target="Cholesky" | custom-call | tf_op jit(solution)/shard_map/while/body/eval_jaxpr/jit(cholesky)/cholesky | solution.py:44
  356.8 2.5 cholesky.254
  359.3 9.8 %custom-call.83 = f32[1,128,128]{1,2,0:T(8,128)S(1)} custom-call(f32[1,128,128]{2,1,0:T(8,128)S(1)} %get-tuple-element.77), custom_call_target="InvertDiagBlocksLowerTriangular" | custom-call | tf_op jit(solution)/shard_map/while/body/eval_jaxpr/jit(cholesky)/cholesky | solution.py:44
  371.9 2.7 convolution_subtract_fusion.1
  374.6 11.7 %cholesky.466 = f32[128,128]{1,0:T(8,128)S(1)} custom-call(f32[128,128]{1,0:T(8,128)S(1)} %cholesky.586), custom_call_target="Cholesky" | custom-call | tf_op jit(solution)/shard_map/while/body/eval_jaxpr/jit(cholesky)/cholesky | solution.py:44
  387.1 9.8 %custom-call.84 = f32[1,128,128]{1,2,0:T(8,128)S(1)} custom-call(f32[1,128,128]{2,1,0:T(8,128)S(1)} %get-tuple-element.75), custom_call_target="InvertDiagBlocksLowerTriangular" | custom-call | tf_op jit(solution)/shard_map/while/body/eval_jaxpr/jit(cholesky)/cholesky | solution.py:44
  398.1 3.3 convolution_subtract_fusion.2
  401.5 11.7 %cholesky.485 = f32[128,128]{1,0:T(8,128)S(1)} custom-call(f32[128,128]{1,0:T(8,128)S(1)} %cholesky.591), custom_call_target="Cholesky" | custom-call | tf_op jit(solution)/shard_map/while/body/eval_jaxpr/jit(cholesky)/cholesky | solution.py:44
  414.0 9.8 %custom-call.85 = f32[1,128,128]{1,2,0:T(8,128)S(1)} custom-call(f32[1,128,128]{2,1,0:T(8,128)S(1)} %get-tuple-element.73), custom_call_target="InvertDiagBlocksLowerTriangular" | custom-call | tf_op jit(solution)/shard_map/while/body/eval_jaxpr/jit(cholesky)/cholesky | solution.py:44
  424.9 3.1 convolution_subtract_fusion.3
  428.1 12.1 %cholesky.504 = f32[128,128]{1,0:T(8,128)S(1)} custom-call(f32[128,128]{1,0:T(8,128)S(1)} %cholesky.596), custom_call_target="Cholesky" | custom-call | tf_op jit(solution)/shard_map/while/body/eval_jaxpr/jit(cholesky)/cholesky | solution.py:44
  440.9 9.8 %custom-call.86 = f32[1,128,128]{1,2,0:T(8,128)S(1)} custom-call(f32[1,128,128]{2,1,0:T(8,128)S(1)} %get-tuple-element.71), custom_call_target="InvertDiagBlocksLowerTriangular" | custom-call | tf_op jit(solution)/shard_map/while/body/eval_jaxpr/jit(cholesky)/cholesky | solution.py:44
  451.9 3.1 convolution_subtract_fusion.4
  455.0 11.7 %cholesky.524 = f32[128,128]{1,0:T(8,128)S(1)} custom-call(f32[128,128]{1,0:T(8,128)S(1)} %cholesky.601), custom_call_target="Cholesky" | custom-call | tf_op jit(solution)/shard_map/while/body/eval_jaxpr/jit(cholesky)/cholesky | solution.py:44
  467.4 9.8 %custom-call.87 = f32[1,128,128]{1,2,0:T(8,128)S(1)} custom-call(f32[1,128,128]{2,1,0:T(8,128)S(1)} %get-tuple-element.69), custom_call_target="InvertDiagBlocksLowerTriangular" | custom-call | tf_op jit(solution)/shard_map/while/body/eval_jaxpr/jit(cholesky)/cholesky | solution.py:44
  478.2 2.8 convolution_subtract_fusion.5
  481.1 11.7 %cholesky.544 = f32[128,128]{1,0:T(8,128)S(1)} custom-call(f32[128,128]{1,0:T(8,128)S(1)} %cholesky.606), custom_call_target="Cholesky" | custom-call | tf_op jit(solution)/shard_map/while/body/eval_jaxpr/jit(cholesky)/cholesky | solution.py:44
  493.6 9.8 %custom-call.88 = f32[1,128,128]{1,2,0:T(8,128)S(1)} custom-call(f32[1,128,128]{2,1,0:T(8,128)S(1)} %get-tuple-element.67), custom_call_target="InvertDiagBlocksLowerTriangular" | custom-call | tf_op jit(solution)/shard_map/while/body/eval_jaxpr/jit(cholesky)/cholesky | solution.py:44
  504.3 2.1 convolution_subtract_fusion.6
  506.4 11.7 %cholesky.562 = f32[128,128]{1,0:T(8,128)S(1)} custom-call(f32[128,128]{1,0:T(8,128)S(1)} %convolution_subtract_fusion.6), custom_call_target="Cholesky" | custom-call | tf_op jit(solution)/shard_map/while/body/eval_jaxpr/jit(cholesky)/cholesky | solution.py:44
  529.2 4.8 select_select_fusion
  534.1 28.5 %while.1 = (s32[]{:T(128)}, f32[1024,1024]{0,1:T(8,128)}, s32[8,2]{0,1:T(2,128)S(1)}, f32[8,128,128]{2,1,0:T(8,128)}, s32[]{:T(128)}) while((s32[]{:T(128)}, f32[1024,1024]{0,1:T(8,128)}, s32[8,2]{0,1:T(2,128)S(1)}, f32[8,128,128]{2,1,0:T(8,128)}, s32[]{:T(128)}) %tuple.66), condition=%wide.while_cond, body=%wide.while_body.sunk | while | flops 2 | bytes 393829 | solution.py:52
  534.7 2.2 dynamic-slice.7
  538.3 2.2 dynamic-slice.7
  541.8 2.2 dynamic-slice.7
  545.4 2.2 dynamic-slice.7
  549.0 2.2 dynamic-slice.7
  552.5 2.2 dynamic-slice.7
  556.1 2.2 dynamic-slice.7
  559.7 2.2 dynamic-slice.7
  562.6 79.6 %custom-call.89 = f32[8,128,128]{1,2,0:T(8,128)S(1)} custom-call(f32[8,128,128]{2,1,0:T(8,128)} %get-tuple-element.27), custom_call_target="InvertDiagBlocksLowerTriangular" | custom-call | tf_op jit(solution)/shard_map/while/body/eval_jaxpr/jit(_solve_triangular)/triangular_solve | solution.py:52
  (177 shorter events, 64.2 us)
Async XLA Ops:
  17.9 7.2 %copy-start.2 = (s32[1,48]{1,0:T(1,128)S(1)}, s32[1,48]{1,0:T(1,128)}, u32[]{:S(2)}) copy-start(s32[1,48]{1,0:T(1,128)} %param.4) | copy-start | bytes 580
  17.9 101.1 %all-to-all-start = ((bf16[2,64,64,512]{3,1,0,2:T(8,128)(2,1)}), bf16[2,64,64,512]{3,1,0,2:T(8,128)(2,1)}, u32[]{:S(2)}, u32[]{:S(2)}) async-start(bf16[2,64,64,512]{3,1,0,2:T(8,128)(2,1)} %copy.107), calls=%async_computation | async-start | bytes 16777216 | tf_op jit(solution)/shard_map/all_to_all | solution.py:88
  150.6 12.0 %copy-start.3 = (s32[1,8]{1,0:T(1,128)S(1)}, s32[1,8]{1,0:T(1,128)}, u32[]{:S(2)}) copy-start(s32[1,8]{1,0:T(1,128)} %param.5) | copy-start | bytes 100
  151.3 7.8 %all-to-all-start.1 = ((bf16[2,2,32,512]{3,2,0,1:T(8,128)(2,1)}), bf16[2,2,32,512]{3,2,0,1:T(8,128)(2,1)S(1)}, u32[]{:S(2)}, u32[]{:S(2)}) async-start(bf16[2,2,32,512]{3,2,0,1:T(8,128)(2,1)} %copy.109), calls=%async_computation.1 | async-start | bytes 262144 | tf_op jit(solution)/shard_map/all_to_all | solution.py:94
  154.6 134.4 %all-gather.3.cloned.1.call-start = ((), (), s32[]{:S(2)}) async-start(), calls=%async_computation.2 | async-start | bytes 17825792 | tf_op jit(solution)/shard_map/all_gather | solution.py:103
  297.1 1.3 copy-start.1
  317.8 1.9 copy-start
Sparse Core Ops, SparseCore 0:
  162.2 126.8 all-gather.2
